TPU v7x, 256 devices: a whole 4x4x8 slice. The times are simulated.
256 devices in a mesh: frames: 4 (over y_lo, core), lon: 64 (over y_hi, x, z).
Axes of the slice: x: 4, y: 4 (y_hi: 2, y_lo: 2; y = y_hi * 2 + y_lo), z: 8, core: 2. Of those that a mesh axis runs over, the one named last changes fastest.
Arguments:
- latents: bfloat16 [32, 2, 1024, 1024], P('frames', None, 'lon'), may hold values from -30 to 30
- window_weight: int32 [32, 64], P('frames'), may hold values from 1 to 8
- modulation: float32 [6, 1024], replicated, may hold values from -4 to 4
- query_spatial: bfloat16 [1024, 512], replicated, may hold values from -2 to 2, as said below
- key_spatial: bfloat16 [1024, 512], replicated, may hold values from -2 to 2, as said below
- value_spatial: bfloat16 [1024, 512], replicated, may hold values from -0.1875 to 0.1875
- out_spatial: bfloat16 [512, 1024], replicated, may hold values from -0.25 to 0.25
- query_temporal: bfloat16 [1024, 512], replicated, may hold values from -2 to 2, as said below
- key_temporal: bfloat16 [1024, 512], replicated, may hold values from -2 to 2, as said below
- value_temporal: bfloat16 [1024, 512], replicated, may hold values from -0.1875 to 0.1875
- out_temporal: bfloat16 [512, 1024], replicated, may hold values from -0.25 to 0.25
Outputs:
- block_output: bfloat16 [32, 2, 1024, 1024], P('frames', None, 'lon')
Inputs may be any that keep to these rules, and one draw needn't show every extreme that they name: `query_spatial`: entries of a projection. `key_spatial`: entries of a projection. `query_temporal`: entries of a projection. `key_temporal`: entries of a projection.
All inputs are finite; a program needn't handle non-finite values.
Results may differ from a plain program's by a relative error of at most 0.0065.
Values may be sent and summed in bfloat16 or wider, within the bound.
No kernel may reach another device: no remote copies, remote signals or barrier semaphores. Data moves between devices by JAX's collectives and lax.ppermute only.
A program may use at most 64 MiB of HBM per device.

v0:
```python
import jax
import jax.numpy as jnp
from jax import lax
from jax.sharding import PartitionSpec as P

HEADS = 8
HD = 64


EPSILON = 1e-06


def padded(cells, sides, width, closed):
    for axis, dim in sides:
        count = lax.axis_size(axis)
        ends = count if closed else count - 1
        head = lax.slice_in_dim(cells, 0, width, axis=dim)
        tail = lax.slice_in_dim(cells, cells.shape[dim] - width, cells.shape[dim], axis=dim)
        cells = jnp.concatenate(
            [
                lax.ppermute(tail, axis, [(i, (i + 1) % count) for i in range(ends)]),
                cells,
                lax.ppermute(head, axis, [((i + 1) % count, i) for i in range(ends)]),
            ],
            axis=dim,
        )
    return cells


def modulate(tokens, shift_row, scale_row):
    values = tokens.astype(jnp.float32)
    centre = jnp.mean(values, axis=-1, keepdims=True)
    centred = values - centre
    spread = jnp.mean(centred * centred, axis=-1, keepdims=True)
    normed = centred * lax.rsqrt(spread + EPSILON)
    return (normed * (1.0 + scale_row) + shift_row).astype(jnp.bfloat16)


def project(inputs, weight):
    return jnp.dot(inputs, weight, preferred_element_type=jnp.float32).astype(jnp.bfloat16)


def attend(queries, key_rows, values, score_form, mix_form):
    factor = queries.shape[-1] ** (-0.5)
    scores = jnp.einsum(score_form, queries, key_rows, preferred_element_type=jnp.float32) * factor
    maximum = jnp.max(scores, axis=-1, keepdims=True)
    raised = jnp.exp(scores - maximum)
    attention = (raised / jnp.sum(raised, axis=-1, keepdims=True)).astype(jnp.bfloat16)
    return jnp.einsum(mix_form, attention, values, preferred_element_type=jnp.float32)


def body(
    latents,
    window_weight,
    modulation,
    query_spatial,
    key_spatial,
    value_spatial,
    out_spatial,
    query_temporal,
    key_temporal,
    value_temporal,
    out_temporal,
):
    frames_here, rows_here, cols_here, _ = latents.shape
    inner_width = query_spatial.shape[1]
    tokens_here = rows_here * cols_here
    normed_space = modulate(latents, modulation[0], modulation[1])
    queries = project(normed_space, query_spatial)
    paired_kv = jnp.stack(
        [project(normed_space, key_spatial), project(normed_space, value_spatial)]
    )
    widened_kv = padded(paired_kv, (("lon", 3),), cols_here, True)
    key_wide = widened_kv[0]
    value_wide = widened_kv[1]
    query_heads = queries.reshape(frames_here, tokens_here, HEADS, HD)

    def window_side(source, offset):
        return source[:, :, offset : offset + 2 * cols_here].reshape(
            frames_here, 2 * tokens_here, HEADS, HD
        )

    west_side = attend(
        query_heads,
        window_side(key_wide, 0),
        window_side(value_wide, 0),
        "bqhe,bkhe->bhqk",
        "bhqk,bkhe->bqhe",
    )
    east_side = attend(
        query_heads,
        window_side(key_wide, cols_here),
        window_side(value_wide, cols_here),
        "bqhe,bkhe->bhqk",
        "bhqk,bkhe->bqhe",
    )
    strip_index = lax.axis_index("lon")
    windows_total = window_weight.shape[1]
    weight_here = lax.dynamic_index_in_dim(window_weight, strip_index, 1, False).astype(
        jnp.float32
    )[:, None, None, None]
    prior_index = (strip_index + windows_total - 1) % windows_total
    weight_prior = lax.dynamic_index_in_dim(window_weight, prior_index, 1, False).astype(
        jnp.float32
    )[:, None, None, None]
    blended = (
        (weight_here * east_side + weight_prior * west_side) / (weight_here + weight_prior)
    ).astype(jnp.bfloat16)
    blended = blended.reshape(frames_here, rows_here, cols_here, inner_width)
    spatial_branch = jnp.dot(blended, out_spatial, preferred_element_type=jnp.float32)
    mixed_tokens = (latents.astype(jnp.float32) + modulation[2] * spatial_branch).astype(
        jnp.bfloat16
    )
    normed_time = modulate(mixed_tokens, modulation[3], modulation[4])
    query_time = project(normed_time, query_temporal)
    key_time = project(normed_time, key_temporal)
    value_time = project(normed_time, value_temporal)
    groups_total = lax.axis_size("frames")
    edged_rows = padded(jnp.stack([key_time, value_time]), (("frames", 1),), frames_here, False)
    query_rows = query_time.reshape(frames_here, tokens_here, HEADS, HD)

    def frame_side(source, offset):
        return source[offset : offset + 2 * frames_here].reshape(
            2 * frames_here, tokens_here, HEADS, HD
        )

    earlier = attend(
        query_rows,
        frame_side(edged_rows[0], 0),
        frame_side(edged_rows[1], 0),
        "qnhe,knhe->nhqk",
        "nhqk,knhe->qnhe",
    )
    later = attend(
        query_rows,
        frame_side(edged_rows[0], frames_here),
        frame_side(edged_rows[1], frames_here),
        "qnhe,knhe->nhqk",
        "nhqk,knhe->qnhe",
    )
    group_index = lax.axis_index("frames")
    has_earlier = (group_index > 0).astype(jnp.float32)
    has_later = (group_index < groups_total - 1).astype(jnp.float32)
    averaged = ((has_earlier * earlier + has_later * later) / (has_earlier + has_later)).astype(
        jnp.bfloat16
    )
    averaged = averaged.reshape(frames_here, rows_here, cols_here, inner_width)
    temporal_branch = jnp.dot(averaged, out_temporal, preferred_element_type=jnp.float32)
    return (mixed_tokens.astype(jnp.float32) + modulation[5] * temporal_branch).astype(jnp.bfloat16)


def solution(mesh):
    return jax.shard_map(
        body,
        mesh=mesh,
        in_specs=(
            P("frames", None, "lon", None),
            P("frames", None),
            P(),
            P(),
            P(),
            P(),
            P(),
            P(),
            P(),
            P(),
            P(),
        ),
        out_specs=P("frames", None, "lon", None),
        check_vma=False,
    )
```

profile of v0, /device:TPU:1, one launch (start us, length us, event | category | flops | bytes accessed | tf_op | source)
XLA Modules:
  0.0 102.3 jit_solution(15449108839701414781)
XLA Ops:
  0.0 1.0 fusion.74
  1.0 1.2 %convert_reduce_fusion.1 = f32[8,2,16]{2,1,0:T(2,128)S(1)} fusion(bf16[8,2,16,1024]{3,2,1,0:T(8,128)(2,1)} %param.11), kind=kLoop, calls=%fused_computation.10 | loop fusion | flops 524032 | bytes 525312 | tf_op jit(solution)/shard_map/reduce_sum | solution.py:32
  2.2 1.3 %fusion.34 = f32[8,2,16]{2,1,0:T(2,128)S(1)} fusion(bf16[8,2,16,1024]{3,2,1,0:T(8,128)(2,1)} %param.11, f32[8,2,16]{2,1,0:T(2,128)S(1)} %broadcast_multiply_fusion.1), kind=kLoop, calls=%fused_computation.57 | loop fusion | flops 1048320 | bytes 526336 | tf_op jit(solution)/shard_map/reduce_sum | solution.py:34
  3.6 2.0 %fusion.27 = bf16[1,8,2,16,512]{4,3,2,1,0:T(8,128)(2,1)S(1)} fusion(bf16[1024,512]{1,0:T(8,128)(2,1)} %param.16, bf16[8,2,16,1024]{3,2,1,0:T(8,128)(2,1)} %param.11, f32[1024]{0:T(1024)S(1)} %bitcast.102, f32[1024]{0:T(1024)S(1)} %bitcast.105, f32[8,2,16]{2,1,0:T(2,128)S(1)} %add_rsqrt_fusion.1, f32[8,2,16]{2,1,0:T(2,128)S(1)} %broadcast_multiply_fusion.1), kind=kOutput, calls=%fused_computation.50 | convolution fusion | flops 270139392 | bytes 1845248 | tf_op jit(solution)/shard_map/dot_general | solution.py:40
  5.6 0.5 fusion.26
  6.2 11.3 %collective-permute-start.1 = (bf16[2,8,2,16,512]{4,3,2,1,0:T(8,128)(2,1)S(1)}, bf16[2,8,2,16,512]{4,3,2,1,0:T(8,128)(2,1)}, u32[]{:S(2)}, u32[]{:S(2)}) collective-permute-start(bf16[2,8,2,16,512]{4,3,2,1,0:T(8,128)(2,1)S(1)} %pad_maximum_fusion.2), channel_id=1, source_target_pairs={{1,0},{2,1},{3,2},{4,3},{5,4},{6,5},{7,6},{8,7},{9,8},{10,9},{11,1... | collective-permute-start | bytes 1572872 | tf_op jit(solution)/shard_map/ppermute | solution.py:23
  17.5 1.7 %convolution_convert_fusion.3 = bf16[8,2,16,512]{3,2,1,0:T(8,128)(2,1)S(1)} fusion(bf16[1024,512]{1,0:T(8,128)(2,1)} %param.14, bf16[8,2,16,1024]{3,2,1,0:T(8,128)(2,1)S(1)} %copy-done.3, f32[1024]{0:T(1024)S(1)} %bitcast.104, f32[1024]{0:T(1024)S(1)} %bitcast.107, f32[8,2,16]{2,1,0:T(2,128)S(1)} %add_rsqrt_fusion.1, ...), kind=kOutput, calls=%fused_computation.46 | convolution fusion | flops 270139392 | bytes 1845248 | tf_op jit(solution)/shard_map/dot_general | solution.py:40
  19.7 8.3 %collective-permute-done.1 = bf16[2,8,2,16,512]{4,3,2,1,0:T(8,128)(2,1)} collective-permute-done((bf16[2,8,2,16,512]{4,3,2,1,0:T(8,128)(2,1)S(1)}, bf16[2,8,2,16,512]{4,3,2,1,0:T(8,128)(2,1)}, u32[]{:S(2)}, u32[]{:S(2)}) %collective-permute-start.1) | collective-permute-done | bytes 524320 | tf_op jit(solution)/shard_map/ppermute | solution.py:23
  28.1 7.7 %collective-permute-done = bf16[2,8,2,16,512]{4,3,2,1,0:T(8,128)(2,1)} collective-permute-done((bf16[2,8,2,16,512]{4,3,2,1,0:T(8,128)(2,1)S(1)}, bf16[2,8,2,16,512]{4,3,2,1,0:T(8,128)(2,1)}, u32[]{:S(2)}, u32[]{:S(2)}) %collective-permute-start) | collective-permute-done | bytes 524320 | tf_op jit(solution)/shard_map/ppermute | solution.py:21
  35.8 1.4 %pad_maximum_fusion = bf16[2,8,2,48,512]{4,3,2,1,0:T(8,128)(2,1)S(1)} fusion(bf16[2,8,2,16,512]{4,3,2,1,0:T(8,128)(2,1)} %collective-permute-done.1, bf16[1,8,2,16,512]{4,3,2,1,0:T(8,128)(2,1)S(1)} %fusion.27, bf16[1,8,2,16,512]{4,3,2,1,0:T(8,128)(2,1)S(1)} %fusion.26, bf16[2,8,2,16,512]{4,3,2,1,0:T(8,128)(2,1)} %collective-permute-done), kind=kLoop, calls=%fused_computation.4 | loop fusion | flops 6291456 | bytes 3145728 | tf_op jit(solution)/shard_map/concatenate | solution.py:19
  37.3 1.2 %fusion.72 = (bf16[8,2,32,512]{3,2,1,0:T(8,128)(2,1)}, bf16[8,2,32,512]{3,2,1,0:T(8,128)(2,1)S(1)}, bf16[8,2,32,512]{3,2,1,0:T(8,128)(2,1)S(1)}, bf16[8,2,32,512]{3,2,1,0:T(8,128)(2,1)}) fusion(bf16[8,2,48,512]{3,2,1,0:T(8,128)(2,1)S(1)} %get-tuple-element.7, bf16[8,2,48,512]{3,2,1,0:T(8,128)(2,1)S(1)} %get-tuple-element.8), kind=kLoop, calls=%fused_computation.107 | loop fusion | bytes 4194304 | tf_op jit(solution)/shard_map/slice | solution.py:79
  38.5 1.5 %reshape.114 = bf16[8,64,8,64]{3,2,1,0:T(8,128)(2,1)} reshape(bf16[8,2,32,512]{3,2,1,0:T(8,128)(2,1)S(1)} %get-tuple-element.31) | data formatting | bytes 1048576 | tf_op jit(solution)/shard_map/reshape | solution.py:79
  40.0 1.6 %reshape.116 = bf16[8,64,8,64]{3,2,1,0:T(8,128)(2,1)} reshape(bf16[8,2,32,512]{3,2,1,0:T(8,128)(2,1)S(1)} %get-tuple-element.14) | data formatting | bytes 1048576 | tf_op jit(solution)/shard_map/reshape | solution.py:79
  41.6 1.9 %convolution_multiply_fusion.7 = f32[8,8,32,64]{3,2,1,0:T(8,128)S(1)} fusion(bf16[8,64,8,64]{3,2,1,0:T(8,128)(2,1)} %reshape.116, bf16[8,32,8,64]{3,2,1,0:T(8,128)(2,1)S(1)} %reshape.115), kind=kOutput, calls=%fused_computation.30 | convolution fusion | flops 16908288 | bytes 1310720 | tf_op jit(solution)/shard_map/bqhe,bkhe->bhqk/dot_general | solution.py:45
  43.5 0.7 fusion.75
  44.2 2.4 %reshape.117 = bf16[8,64,8,64]{3,2,1,0:T(8,128)(2,1)} reshape(bf16[8,2,32,512]{3,2,1,0:T(8,128)(2,1)} %get-tuple-element.32) | data formatting | bytes 1048576 | tf_op jit(solution)/shard_map/reshape | solution.py:79
  46.6 2.4 %reshape.118 = bf16[8,64,8,64]{3,2,1,0:T(8,128)(2,1)} reshape(bf16[8,2,32,512]{3,2,1,0:T(8,128)(2,1)} %get-tuple-element.13) | data formatting | bytes 1048576 | tf_op jit(solution)/shard_map/reshape | solution.py:79
  49.0 1.9 %convolution_multiply_fusion.6 = f32[8,8,32,64]{3,2,1,0:T(8,128)S(1)} fusion(bf16[8,64,8,64]{3,2,1,0:T(8,128)(2,1)} %reshape.118, bf16[8,32,8,64]{3,2,1,0:T(8,128)(2,1)S(1)} %reshape.115), kind=kOutput, calls=%fused_computation.29 | convolution fusion | flops 16908288 | bytes 1310720 | tf_op jit(solution)/shard_map/bqhe,bkhe->bhqk/dot_general | solution.py:45
  50.9 1.0 copy-done.2
  51.8 0.7 fusion.76
  52.5 5.9 %convolution_multiply_fusion.1 = f32[8,8,64,32]{2,3,1,0:T(8,128)} fusion(bf16[8,64,8,64]{3,2,1,0:T(8,128)(2,1)} %reshape.114, f32[8,8,32]{2,1,0:T(8,128)S(1)} %fusion.75, f32[8]{0:T(128)S(1)} %get-tuple-element.6, f32[8,8,32,64]{3,2,1,0:T(8,128)S(1)} %convolution_multiply_fusion.7), kind=kOutput, calls=%fused_computation.22 | convolution fusion | flops 17303616 | bytes 1581088 | tf_op jit(solution)/shard_map/bhqk,bkhe->bqhe/dot_general | solution.py:49
  58.4 5.9 %fusion.24 = bf16[8,32,8,64]{3,1,2,0:T(8,128)(2,1)S(1)} fusion(f32[8,8,64,32]{2,3,1,0:T(8,128)} %convolution_multiply_fusion.1, bf16[8,64,8,64]{3,2,1,0:T(8,128)(2,1)} %reshape.117, f32[8]{0:T(128)S(1)} %add.106, f32[8,8,32]{2,1,0:T(8,128)S(1)} %fusion.76, f32[8]{0:T(128)S(1)} %get-tuple-element.5, f32[8,8,32,64]{3,2,1,0:T(8,128)} %copy-done.2), kind=kOutput, calls=%fused_computation.41 | convolution fusion | flops 17696832 | bytes 1843264 | tf_op jit(solution)/shard_map/bhqk,bkhe->bqhe/dot_general | solution.py:49
  64.5 0.3 reshape.119
  64.9 0.5 convert_reduce_fusion
  65.7 0.3 copy-done.13
  66.1 0.5 fusion.29
  66.6 0.4 copy-done.14
  67.0 0.5 fusion.28
  67.6 3.7 %collective-permute-start.3 = (bf16[2,8,2,16,512]{4,3,2,1,0:T(8,128)(2,1)S(1)}, bf16[2,8,2,16,512]{4,3,2,1,0:T(8,128)(2,1)S(1)}, u32[]{:S(2)}, u32[]{:S(2)}) collective-permute-start(bf16[2,8,2,16,512]{4,3,2,1,0:T(8,128)(2,1)S(1)} %pad_maximum_fusion.3), channel_id=1, source_target_pairs={{64,0},{128,64},{192,128},{65,1},{129,65},{193,129},{66,2},{130,66... | collective-permute-start | bytes 1572872 | tf_op jit(solution)/shard_map/ppermute | solution.py:23
  71.3 2.4 %collective-permute-start.2 = (bf16[2,8,2,16,512]{4,3,2,1,0:T(8,128)(2,1)S(1)}, bf16[2,8,2,16,512]{4,3,2,1,0:T(8,128)(2,1)}, u32[]{:S(2)}, u32[]{:S(2)}) collective-permute-start(bf16[2,8,2,16,512]{4,3,2,1,0:T(8,128)(2,1)S(1)} %pad_maximum_fusion.3), channel_id=1, source_target_pairs={{0,64},{64,128},{128,192},{1,65},{65,129},{129,193},{2,66},{66,130... | collective-permute-start | bytes 1572872 | tf_op jit(solution)/shard_map/ppermute | solution.py:21
  73.8 1.7 %convolution_convert_fusion = bf16[8,2,16,512]{3,2,1,0:T(8,128)(2,1)S(1)} fusion(bf16[1024,512]{1,0:T(8,128)(2,1)} %param.18, bf16[8,2,16,1024]{3,2,1,0:T(8,128)(2,1)S(1)} %get-tuple-element.26, f32[1024]{0:T(1024)S(1)} %bitcast.97, f32[1024]{0:T(1024)S(1)} %bitcast.100, f32[8,2,16]{2,1,0:T(2,128)S(1)} %add_rsqrt_fusion, ...), kind=kOutput, calls=%fused_computation.43 | convolution fusion | flops 270139392 | bytes 1845248 | tf_op jit(solution)/shard_map/dot_general | solution.py:40
  75.8 2.7 %collective-permute-done.3 = bf16[2,8,2,16,512]{4,3,2,1,0:T(8,128)(2,1)S(1)} collective-permute-done((bf16[2,8,2,16,512]{4,3,2,1,0:T(8,128)(2,1)S(1)}, bf16[2,8,2,16,512]{4,3,2,1,0:T(8,128)(2,1)S(1)}, u32[]{:S(2)}, u32[]{:S(2)}) %collective-permute-start.3) | collective-permute-done | bytes 524320 | tf_op jit(solution)/shard_map/ppermute | solution.py:23
  78.4 0.8 copy-done.10
  79.2 0.4 collective-permute-done.2
  79.6 1.4 %pad_maximum_fusion.1 = (bf16[2,16,2,16,512]{4,3,2,1,0:T(8,128)(2,1)S(1)}, bf16[2,16,2,16,512]{4,3,2,1,0:T(8,128)(2,1)S(1)}) fusion(bf16[2,8,2,16,512]{4,3,2,1,0:T(8,128)(2,1)} %copy-done.10, bf16[1,8,2,16,512]{4,3,2,1,0:T(8,128)(2,1)S(1)} %fusion.29, bf16[1,8,2,16,512]{4,3,2,1,0:T(8,128)(2,1)S(1)} %fusion.28, ...), kind=kLoop, calls=%fused_computation.62 | loop fusion | flops 2097152 | bytes 3670016 | tf_op jit(solution)/shard_map/concatenate | solution.py:19
  81.0 0.9 fusion.71
  81.9 2.4 %reshape.120 = bf16[16,32,8,64]{3,2,1,0:T(8,128)(2,1)} reshape(bf16[1,16,2,16,512]{4,3,2,1,0:T(8,128)(2,1)} %get-tuple-element.12) | data formatting | bytes 1048576 | tf_op jit(solution)/shard_map/reshape | solution.py:123
  84.3 1.5 %reshape.122 = bf16[16,32,8,64]{3,2,1,0:T(8,128)(2,1)} reshape(bf16[1,16,2,16,512]{4,3,2,1,0:T(8,128)(2,1)S(1)} %get-tuple-element.11) | data formatting | bytes 1048576 | tf_op jit(solution)/shard_map/reshape | solution.py:123
  85.8 0.9 fusion.70
  86.7 2.5 %reshape.123 = bf16[16,32,8,64]{3,2,1,0:T(8,128)(2,1)} reshape(bf16[1,16,2,16,512]{4,3,2,1,0:T(8,128)(2,1)} %get-tuple-element.10) | data formatting | bytes 1048576 | tf_op jit(solution)/shard_map/reshape | solution.py:123
  89.2 1.5 %reshape.124 = bf16[16,32,8,64]{3,2,1,0:T(8,128)(2,1)} reshape(bf16[1,16,2,16,512]{4,3,2,1,0:T(8,128)(2,1)S(1)} %get-tuple-element.9) | data formatting | bytes 1048576 | tf_op jit(solution)/shard_map/reshape | solution.py:123
  90.7 2.2 %fusion.77 = (f32[32,8,8]{2,1,0:T(8,128)S(1)}, f32[32,8,8,16]{3,2,1,0:T(8,128)}) fusion(bf16[16,32,8,64]{3,2,1,0:T(8,128)(2,1)S(1)} %copy-done.1, bf16[8,32,8,64]{3,2,1,0:T(8,128)(2,1)S(1)} %reshape.121), kind=kOutput, calls=%fused_computation.112 | convolution fusion | flops 4292623 | bytes 925696 | tf_op jit(solution)/shard_map/sub | solution.py:47
  93.0 3.6 %fusion.78 = (f32[32,8,8]{2,1,0:T(8,128)S(1)}, f32[32,8,8,16]{3,2,1,0:T(8,128)}) fusion(bf16[16,32,8,64]{3,2,1,0:T(8,128)(2,1)} %reshape.124, bf16[8,32,8,64]{3,2,1,0:T(8,128)(2,1)S(1)} %reshape.121), kind=kOutput, calls=%fused_computation.113 | convolution fusion | flops 4292623 | bytes 925696 | tf_op jit(solution)/shard_map/sub | solution.py:47
  96.5 2.2 %convolution_multiply_fusion.4 = f32[32,8,64,8]{2,3,1,0:T(8,128)S(1)} fusion(bf16[16,32,8,64]{3,2,1,0:T(8,128)(2,1)S(1)} %copy-done.6, f32[32,8,8,16]{3,2,1,0:T(8,128)} %get-tuple-element.28, f32[32,8,8]{2,1,0:T(8,128)S(1)} %get-tuple-element.27, f32[]{:T(128)S(6)} %convert_element_type.109), kind=kOutput, calls=%fused_computation.27 | convolution fusion | flops 4390912 | bytes 1187844 | tf_op jit(solution)/shard_map/nhqk,knhe->qnhe/dot_general | solution.py:49
  98.7 0.9 fusion.25
  100.0 0.6 copy-done.5
  100.7 0.3 copy-done.8
  101.0 1.2 %fusion.19 = bf16[8,2,16,1024]{3,2,1,0:T(8,128)(2,1)} fusion(bf16[8,2,16,512]{3,2,1,0:T(8,128)(2,1)S(1)} %reshape.125, bf16[8,2,16,1024]{3,2,1,0:T(8,128)(2,1)S(1)} %copy-done.5, bf16[512,1024]{1,0:T(8,128)(2,1)S(1)} %copy-done.8, f32[1024]{0:T(1024)S(1)} %bitcast.94), kind=kOutput, calls=%fused_computation.36 | convolution fusion | flops 269484032 | bytes 2363392 | tf_op jit(solution)/shard_map/dot_general | solution.py:148
  (40 shorter events, 2.0 us)
Async XLA Ops:
  0.0 64.8 %copy-start = (bf16[512,1024]{1,0:T(8,128)(2,1)S(1)}, bf16[512,1024]{1,0:T(8,128)(2,1)}, u32[]{:S(2)}) copy-start(bf16[512,1024]{1,0:T(8,128)(2,1)} %param.17) | copy-start | bytes 3145732
  3.5 2.0 %copy-start.3 = (bf16[8,2,16,1024]{3,2,1,0:T(8,128)(2,1)S(1)}, bf16[8,2,16,1024]{3,2,1,0:T(8,128)(2,1)}, u32[]{:S(2)}) copy-start(bf16[8,2,16,1024]{3,2,1,0:T(8,128)(2,1)} %param.11) | copy-start | bytes 1572868
  3.6 2.0 %copy-start.12 = (bf16[1024,512]{1,0:T(8,128)(2,1)S(1)}, bf16[1024,512]{1,0:T(8,128)(2,1)}, u32[]{:S(2)}) copy-start(bf16[1024,512]{1,0:T(8,128)(2,1)} %param.15) | copy-start | bytes 3145732
  6.2 21.9 %collective-permute-start.1 = (bf16[2,8,2,16,512]{4,3,2,1,0:T(8,128)(2,1)S(1)}, bf16[2,8,2,16,512]{4,3,2,1,0:T(8,128)(2,1)}, u32[]{:S(2)}, u32[]{:S(2)}) collective-permute-start(bf16[2,8,2,16,512]{4,3,2,1,0:T(8,128)(2,1)S(1)} %pad_maximum_fusion.2), channel_id=1, source_target_pairs={{1,0},{2,1},{3,2},{4,3},{5,4},{6,5},{7,6},{8,7},{9,8},{10,9},{11,1... | collective-permute-start | bytes 1572872 | tf_op jit(solution)/shard_map/ppermute | solution.py:23
  17.5 18.3 %collective-permute-start = (bf16[2,8,2,16,512]{4,3,2,1,0:T(8,128)(2,1)S(1)}, bf16[2,8,2,16,512]{4,3,2,1,0:T(8,128)(2,1)}, u32[]{:S(2)}, u32[]{:S(2)}) collective-permute-start(bf16[2,8,2,16,512]{4,3,2,1,0:T(8,128)(2,1)S(1)} %pad_maximum_fusion.2), channel_id=1, source_target_pairs={{0,1},{1,2},{2,3},{3,4},{4,5},{5,6},{6,7},{7,8},{8,9},{9,10},{10,1... | collective-permute-start | bytes 1572872 | tf_op jit(solution)/shard_map/ppermute | solution.py:21
  17.5 2.0 %copy-start.11 = (s32[8,64]{1,0:T(8,128)S(1)}, s32[8,64]{1,0:T(8,128)}, u32[]{:S(2)}) copy-start(s32[8,64]{1,0:T(8,128)} %param.12) | copy-start | bytes 6148
  50.9 1.0 copy-start.2
  64.8 1.2 %copy-start.13 = (bf16[1024,512]{1,0:T(8,128)(2,1)S(1)}, bf16[1024,512]{1,0:T(8,128)(2,1)}, u32[]{:S(2)}) copy-start(bf16[1024,512]{1,0:T(8,128)(2,1)} %param.20) | copy-start | bytes 3145732
  65.4 8.4 %copy-start.4 = (bf16[8,2,16,1024]{3,2,1,0:T(8,128)(2,1)}, bf16[8,2,16,1024]{3,2,1,0:T(8,128)(2,1)S(1)}, u32[]{:S(2)}) copy-start(bf16[8,2,16,1024]{3,2,1,0:T(8,128)(2,1)S(1)} %get-tuple-element.26) | copy-start | bytes 1572868
  65.7 1.3 %copy-start.14 = (bf16[1024,512]{1,0:T(8,128)(2,1)S(1)}, bf16[1024,512]{1,0:T(8,128)(2,1)}, u32[]{:S(2)}) copy-start(bf16[1024,512]{1,0:T(8,128)(2,1)} %param.19) | copy-start | bytes 3145732
  67.6 10.9 %collective-permute-start.3 = (bf16[2,8,2,16,512]{4,3,2,1,0:T(8,128)(2,1)S(1)}, bf16[2,8,2,16,512]{4,3,2,1,0:T(8,128)(2,1)S(1)}, u32[]{:S(2)}, u32[]{:S(2)}) collective-permute-start(bf16[2,8,2,16,512]{4,3,2,1,0:T(8,128)(2,1)S(1)} %pad_maximum_fusion.3), channel_id=1, source_target_pairs={{64,0},{128,64},{192,128},{65,1},{129,65},{193,129},{66,2},{130,66... | collective-permute-start | bytes 1572872 | tf_op jit(solution)/shard_map/ppermute | solution.py:23
  71.3 8.3 %collective-permute-start.2 = (bf16[2,8,2,16,512]{4,3,2,1,0:T(8,128)(2,1)S(1)}, bf16[2,8,2,16,512]{4,3,2,1,0:T(8,128)(2,1)}, u32[]{:S(2)}, u32[]{:S(2)}) collective-permute-start(bf16[2,8,2,16,512]{4,3,2,1,0:T(8,128)(2,1)S(1)} %pad_maximum_fusion.3), channel_id=1, source_target_pairs={{0,64},{64,128},{128,192},{1,65},{65,129},{129,193},{2,66},{66,130... | collective-permute-start | bytes 1572872 | tf_op jit(solution)/shard_map/ppermute | solution.py:21
  78.4 0.8 copy-start.10
  86.7 4.0 %copy-start.1 = (bf16[16,32,8,64]{3,2,1,0:T(8,128)(2,1)S(1)}, bf16[16,32,8,64]{3,2,1,0:T(8,128)(2,1)}, u32[]{:S(2)}) copy-start(bf16[16,32,8,64]{3,2,1,0:T(8,128)(2,1)} %reshape.122) | copy-start | bytes 1572868
  93.0 3.6 %copy-start.6 = (bf16[16,32,8,64]{3,2,1,0:T(8,128)(2,1)S(1)}, bf16[16,32,8,64]{3,2,1,0:T(8,128)(2,1)}, u32[]{:S(2)}) copy-start(bf16[16,32,8,64]{3,2,1,0:T(8,128)(2,1)} %reshape.120) | copy-start | bytes 1572868
  96.5 2.2 %copy-start.7 = (bf16[16,32,8,64]{3,2,1,0:T(8,128)(2,1)S(1)}, bf16[16,32,8,64]{3,2,1,0:T(8,128)(2,1)}, u32[]{:S(2)}) copy-start(bf16[16,32,8,64]{3,2,1,0:T(8,128)(2,1)} %reshape.123) | copy-start | bytes 1572868
  96.5 2.2 %copy-start.9 = (f32[32,8,8,16]{3,2,1,0:T(8,128)S(1)}, f32[32,8,8,16]{3,2,1,0:T(8,128)}, u32[]{:S(2)}) copy-start(f32[32,8,8,16]{3,2,1,0:T(8,128)} %get-tuple-element.30) | copy-start | bytes 393220
  99.6 1.0 %copy-start.5 = (bf16[8,2,16,1024]{3,2,1,0:T(8,128)(2,1)S(1)}, bf16[8,2,16,1024]{3,2,1,0:T(8,128)(2,1)}, u32[]{:S(2)}) copy-start(bf16[8,2,16,1024]{3,2,1,0:T(8,128)(2,1)} %copy-done.4) | copy-start | bytes 1572868
  99.6 1.4 %copy-start.8 = (bf16[512,1024]{1,0:T(8,128)(2,1)S(1)}, bf16[512,1024]{1,0:T(8,128)(2,1)}, u32[]{:S(2)}) copy-start(bf16[512,1024]{1,0:T(8,128)(2,1)} %param.21) | copy-start | bytes 3145732
where the time goes:
time: 103 us; the launch traced here: 102 us
  matrix products  33.1 us (32%)
  local copies, waits for them, and re-layouts  24 us (23%)
  waiting for transfers between devices  19.1 us (19%)
  starting transfers between devices  17.5 us (17%)
  other arithmetic  8.24 us (8%)
    ppermute x2, starting transfers between devices, padded(): lax.ppermute(head, axis, [((i + 1) % count, i) for i in range(ends)])  15 us
    dot_general x4, matrix products, attend(): jnp.einsum(mix_form, attention, values, preferred_element_type=jnp.float32)  14.8 us
    ppermute x2, waiting for transfers between devices, padded(): lax.ppermute(head, axis, [((i + 1) % count, i) for i in range(ends)])  11 us
    ppermute x2, waiting for transfers between devices, padded(): lax.ppermute(tail, axis, [(i, (i + 1) % count) for i in range(ends)])  8.14 us
    reshape x4, local copies, waits for them, and re-layouts, frame_side(): source[offset:offset + 2 * frames_here]  7.94 us
    reshape x4, local copies, waits for them, and re-layouts, window_side(): source[:, :, offset:offset + 2 * cols_here]  7.92 us
    dot_general x6, matrix products, project(): jnp.dot(inputs, weight, preferred_element_type=jnp.float32)  6.93 us
    sub x2, matrix products, attend(): raised = jnp.exp(scores - maximum)  5.81 us
  transfers between devices with their start and end apart: 4, of which 4 were waited for; matrix products, arithmetic and copies ran while one was open for 4% of the time, Pallas kernels for 0%

commit v1 on v0

v1 whole, which is shorter than its diff:
```python
import functools

import jax
import jax.numpy as jnp
from jax import lax
from jax.experimental import pallas as pl
from jax.experimental.pallas import tpu as pltpu
from jax.sharding import PartitionSpec as P


HEADS = 8
HD = 64
D = 1024
HW = 512
F = 8
R = 2
C = 16
TOK = F * R * C
NCH = 2
FC = F // NCH
BLK = 128
EPSILON = 1e-06
NEG = -1e30
MIB = 1024 * 1024


VM = pl.BlockSpec(memory_space=pltpu.VMEM)
HBM = pl.BlockSpec(memory_space=pltpu.HBM)


def f32dot(a, b):
    return jnp.dot(a, b, preferred_element_type=jnp.float32)


def modulate(values, shift_row, scale_row):
    centre = jnp.mean(values, axis=-1, keepdims=True)
    centred = values - centre
    spread = jnp.mean(centred * centred, axis=-1, keepdims=True)
    normed = centred * lax.rsqrt(spread + EPSILON)
    return (normed * (1.0 + scale_row) + shift_row).astype(jnp.bfloat16)


def mixed_heads(q, keys, values, bias, share_a, share_b):
    half = lax.broadcasted_iota(jnp.int32, (BLK, BLK), 1) < HD
    zero = jnp.zeros((BLK, BLK), jnp.bfloat16)
    ones = jnp.ones((2 * BLK, BLK), jnp.bfloat16)
    pieces = []
    for pair in range(HEADS // 2):
        lanes = slice(pair * BLK, (pair + 1) * BLK)
        qp = q[:, lanes]
        stacked = jnp.concatenate([jnp.where(half, qp, zero), jnp.where(half, zero, qp)], axis=0)
        kc = jnp.concatenate([k[:, lanes] for k in keys], axis=0)
        scores = lax.dot_general(
            stacked, kc, (((1,), (1,)), ((), ())), preferred_element_type=jnp.float32
        )
        scores = scores + bias
        total = None
        for first, share in ((0, share_a), (1, share_b)):
            window = scores[:, first * BLK : (first + 2) * BLK]
            top = jnp.max(window, axis=-1, keepdims=True)
            raised = jnp.exp(window - top).astype(jnp.bfloat16)
            vc = jnp.concatenate([values[first][:, lanes], values[first + 1][:, lanes]], axis=0)
            mix = f32dot(raised, jnp.concatenate([vc, ones], axis=1))
            part = mix[:, :BLK] * (share / mix[:, BLK:])
            total = part if total is None else total + part
        pieces.append(jnp.where(half, total[:BLK], total[BLK:]))
    return jnp.concatenate(pieces, axis=1).astype(jnp.bfloat16)


def block_bias(key_of):
    row = lax.broadcasted_iota(jnp.int32, (2 * BLK, 3 * BLK), 0)
    col = lax.broadcasted_iota(jnp.int32, (2 * BLK, 3 * BLK), 1)
    return jnp.where(key_of(row) == key_of(col), 0.0, NEG)


def frame_shares(weight_ref, frame):
    count = weight_ref.shape[1]
    strip = lax.axis_index("lon")
    weights = weight_ref[...].astype(jnp.float32)
    spot = lax.broadcasted_iota(jnp.int32, weights.shape, 1)
    here = jnp.sum(jnp.where(spot == strip, weights, 0.0), axis=1, keepdims=True)
    prior = jnp.sum(
        jnp.where(spot == lax.rem(strip + count - 1, count), weights, 0.0), axis=1, keepdims=True
    )
    share = here / (here + prior)
    rows = [
        jnp.broadcast_to(share[f : f + 1], (R * C, 1))
        for f in range(frame, frame + BLK // (R * C))
    ]
    return jnp.concatenate(rows + rows, axis=0)


def own_kernel(*refs):
    mod_ref, x_hbm, wq_hbm = refs[:3]
    stored_hbm = refs[3:10]
    x_ref, q_ref, k_ref, v_ref = refs[10:14]
    stored = refs[14:21]
    wq_ref, sem = refs[21:]
    copies = [
        pltpu.make_async_copy(src, dst, sem.at[i])
        for i, (src, dst) in enumerate(
            zip((x_hbm, wq_hbm) + stored_hbm, (x_ref, wq_ref) + stored)
        )
    ]
    for copy in copies:
        copy.start()
    copies[0].wait()
    blocks = [slice(i * BLK, (i + 1) * BLK) for i in range(TOK // BLK)]
    normed = [
        modulate(x_ref[rows].astype(jnp.float32), mod_ref[0:1], mod_ref[1:2]) for rows in blocks
    ]
    copies[1].wait()
    for rows, n in zip(blocks, normed):
        q_ref[rows] = (f32dot(n, wq_ref[...]).astype(jnp.bfloat16) * HD**-0.5).astype(jnp.bfloat16)
    copies[2].wait()
    for rows, n in zip(blocks, normed):
        k_ref[rows] = f32dot(n, stored[0][...]).astype(jnp.bfloat16)
    copies[3].wait()
    for rows, n in zip(blocks, normed):
        v_ref[rows] = f32dot(n, stored[1][...]).astype(jnp.bfloat16)
    for copy in copies[4:]:
        copy.wait()


def split_kernel(x_hbm, *refs):
    sem = refs[-1]
    rows = TOK // NCH
    copies = [
        pltpu.make_async_copy(x_hbm.at[pl.ds(i * rows, rows)], refs[i], sem.at[i])
        for i in range(NCH)
    ]
    for copy in copies:
        copy.start()
    for copy in copies:
        copy.wait()


def space_kernel(
    base,
    west_ref,
    east_ref,
    x_ref,
    q_ref,
    k_ref,
    v_ref,
    weight_ref,
    mod_ref,
    wk_ref,
    wv_ref,
    wo_ref,
    wqt_ref,
    wkt_ref,
    wvt_ref,
    mixed_ref,
    qt_ref,
    kvt_ref,
):
    bias = block_bias(lambda i: (i & (BLK - 1)) >> 5)
    for i in range(west_ref.shape[0] // BLK):
        here = slice(i * BLK, (i + 1) * BLK)
        rows = slice(base + i * BLK, base + (i + 1) * BLK)
        sides = []
        for ref in (west_ref, east_ref):
            n = modulate(ref[here].astype(jnp.float32), mod_ref[0:1], mod_ref[1:2])
            sides.append(
                (
                    f32dot(n, wk_ref[...]).astype(jnp.bfloat16),
                    f32dot(n, wv_ref[...]).astype(jnp.bfloat16),
                )
            )
        share = frame_shares(weight_ref, (base + i * BLK) // (R * C))
        blended = mixed_heads(
            q_ref[rows],
            (sides[0][0], k_ref[rows], sides[1][0]),
            (sides[0][1], v_ref[rows], sides[1][1]),
            bias,
            1.0 - share,
            share,
        )
        branch = f32dot(blended, wo_ref[...])
        mixed = (x_ref[rows].astype(jnp.float32) + mod_ref[2:3] * branch).astype(jnp.bfloat16)
        mixed_ref[here] = mixed
        n = modulate(mixed.astype(jnp.float32), mod_ref[3:4], mod_ref[4:5])
        kvt_ref[here, :HW] = f32dot(n, wkt_ref[...]).astype(jnp.bfloat16)
        kvt_ref[here, HW:] = f32dot(n, wvt_ref[...]).astype(jnp.bfloat16)
        qt_ref[here] = (f32dot(n, wqt_ref[...]).astype(jnp.bfloat16) * HD**-0.5).astype(
            jnp.bfloat16
        )


def time_kernel(*refs):
    mod_ref, wo_ref = refs[:2]
    chunks = [refs[2 + 5 * i : 7 + 5 * i] for i in range(NCH)]
    group = lax.axis_index("frames")
    paired = jnp.where(
        jnp.logical_and(group > 0, group < lax.axis_size("frames") - 1), 0.5, 0.0
    )
    out_ref = refs[-1]
    bias = block_bias(lambda i: i & (C - 1))
    for r in range(R):

        def rows_of(slot, lanes):
            return jnp.concatenate(
                [
                    refs_here[slot][f * R * C + r * C : f * R * C + (r + 1) * C, lanes]
                    for refs_here in chunks
                    for f in range(FC)
                ],
                axis=0,
            )

        first, second, whole = slice(0, HW), slice(HW, 2 * HW), slice(0, D)
        blended = mixed_heads(
            rows_of(0, first),
            (rows_of(2, first), rows_of(1, first), rows_of(3, first)),
            (rows_of(2, second), rows_of(1, second), rows_of(3, second)),
            bias,
            1.0 - paired,
            paired,
        )
        branch = f32dot(blended, wo_ref[...])
        out = (rows_of(4, whole).astype(jnp.float32) + mod_ref[5:6] * branch).astype(jnp.bfloat16)
        for f in range(F):
            out_ref[f * R * C + r * C : f * R * C + (r + 1) * C] = out[f * C : (f + 1) * C]


def body(
    latents,
    window_weight,
    modulation,
    query_spatial,
    key_spatial,
    value_spatial,
    out_spatial,
    query_temporal,
    key_temporal,
    value_temporal,
    out_temporal,
):
    strips = lax.axis_size("lon")
    bf = jnp.bfloat16
    x = latents.reshape(TOK, D)
    rows = TOK // NCH
    forward = [(i, (i + 1) % strips) for i in range(strips)]
    back = [((i + 1) % strips, i) for i in range(strips)]
    shape = jax.ShapeDtypeStruct

    def keep(array):
        return pltpu.with_memory_space_constraint(array, pltpu.HBM)

    if NCH > 1:
        chunks = pl.pallas_call(
            split_kernel,
            out_shape=[shape((rows, D), bf)] * NCH,
            in_specs=[HBM],
            out_specs=[VM] * NCH,
            scratch_shapes=[pltpu.SemaphoreType.DMA((NCH,))],
            compiler_params=pltpu.CompilerParams(vmem_limit_bytes=4 * MIB),
            name="split",
        )(keep(x))
    else:
        chunks = [x]
    west, east = [], []
    for i in range(NCH):
        west.append(lax.ppermute(chunks[i], "lon", forward))
    for i in range(NCH):
        east.append(lax.ppermute(chunks[i], "lon", back))

    wide, tall = shape((D, HW), bf), shape((HW, D), bf)
    stored = pl.pallas_call(
        own_kernel,
        out_shape=[shape((TOK, D), bf)]
        + [shape((TOK, HW), bf)] * 3
        + [wide, wide, tall, wide, wide, wide, tall],
        in_specs=[VM] + [HBM] * 9,
        out_specs=[VM] * 11,
        scratch_shapes=[pltpu.VMEM((D, HW), bf), pltpu.SemaphoreType.DMA((9,))],
        compiler_params=pltpu.CompilerParams(vmem_limit_bytes=24 * MIB),
        name="own",
    )(
        modulation,
        *map(
            keep,
            (
                x,
                query_spatial,
                key_spatial,
                value_spatial,
                out_spatial,
                query_temporal,
                key_temporal,
                value_temporal,
                out_temporal,
            ),
        ),
    )
    own, weights, out_weight = stored[:4], stored[4:10], stored[10]
    time_args = []
    for i in range(NCH):
        mixed, qt, kvt = pl.pallas_call(
            functools.partial(space_kernel, i * rows),
            out_shape=[shape((rows, D), bf), shape((rows, HW), bf), shape((rows, D), bf)],
            in_specs=[VM] * 14,
            out_specs=[VM] * 3,
            compiler_params=pltpu.CompilerParams(vmem_limit_bytes=20 * MIB),
        )(west[i], east[i], *own, window_weight, modulation, *weights)
        cross = lax.ppermute(kvt, "frames", [(1, 2), (2, 1)])
        mate = lax.ppermute(kvt, "frames", [(0, 1), (1, 0), (2, 3), (3, 2)])
        time_args += [qt, kvt, mate, cross, mixed]

    out = pl.pallas_call(
        time_kernel,
        out_shape=shape((TOK, D), bf),
        in_specs=[VM] * (2 + len(time_args)),
        out_specs=VM,
        compiler_params=pltpu.CompilerParams(vmem_limit_bytes=20 * MIB),
        name="time",
    )(modulation, out_weight, *time_args)
    return out.reshape(latents.shape)


def solution(mesh):
    return jax.shard_map(
        body,
        mesh=mesh,
        in_specs=(P("frames", None, "lon", None), P("frames", None)) + (P(),) * 9,
        out_specs=P("frames", None, "lon", None),
        check_vma=False,
    )
```

time: 103 us -> 47.8 us (0.46)
  matrix products: 33.1 us -> 0 us
  local copies, waits for them, and re-layouts: 24 us -> 0.69 us
  Pallas kernels: 0 us -> 14.8 us
  waiting for transfers between devices: 19.1 us -> 5.98 us
  starting transfers between devices: 17.5 us -> 26 us
  other arithmetic: 8.24 us -> 0 us
    dot_general x14 -> x0, matrix products: 27.3 us -> none  [the longest x4 14.8 us: attend(): jnp.einsum(mix_form, attention, values, preferred_element_type=jnp.float32)]
    reshape x12 -> x0, local copies, waits for them, and re-layouts: 17 us -> none  [the longest x4 7.94 us: frame_side(): source[offset:offset + 2 * frames_here]]
    pallas_call x0 -> x5, Pallas kernels: none -> 14.8 us  [the longest x2 6.33 us: body(): pl.pallas_call(functools.partial(space_kernel, i * rows), out_shape=[shap...]
    ppermute x4 -> x8, waiting for transfers between devices: 19.1 us -> 5.98 us  [the longest x2 4.18 us: body(): cross = lax.ppermute(kvt, 'frames', [(1, 2), (2, 1)])]
    ppermute x4 -> x8, starting transfers between devices: 17.5 us -> 26 us  [the longest x2 18.5 us: body(): east.append(lax.ppermute(chunks[i], 'lon', back))]
    sub x2 -> x0, matrix products: 5.81 us -> none  [attend(): raised = jnp.exp(scores - maximum)]
    slice x3 -> x0, local copies, waits for them, and re-layouts: 3 us -> none  [the longest x2 1.78 us: frame_side(): source[offset:offset + 2 * frames_here]]
    unnamed x30 -> x4, local copies, waits for them, and re-layouts: 3.57 us -> 0.69 us
  transfers between devices with their start and end apart: 4 -> 8, of which waited for: 4 -> 2; matrix products, arithmetic and copies ran while one was open for 4% -> 0% of each run, Pallas kernels for 0% -> 21%
where the time goes in v1:
time: 47.8 us; the launch traced here: 47.6 us
  starting transfers between devices  26 us (54%)
  Pallas kernels  14.8 us (31%)
  waiting for transfers between devices  5.98 us (13%)
  local copies, waits for them, and re-layouts  0.69 us (1%)
    ppermute x2, starting transfers between devices, body(): east.append(lax.ppermute(chunks[i], 'lon', back))  18.5 us
    ppermute x2, starting transfers between devices, body(): cross = lax.ppermute(kvt, 'frames', [(1, 2), (2, 1)])  7.2 us
    pallas_call x2, Pallas kernels, body(): pl.pallas_call(functools.partial(space_kernel, i * rows), out_shape=[shap...  6.33 us
    ppermute x2, waiting for transfers between devices, body(): cross = lax.ppermute(kvt, 'frames', [(1, 2), (2, 1)])  4.18 us
    pallas_call x1, Pallas kernels, body(): pl.pallas_call(time_kernel, out_shape=shape((TOK, D), bf), in_specs=[VM]...  3.8 us
    pallas_call x1, Pallas kernels, body(): pl.pallas_call(own_kernel, out_shape=[shape((TOK, D), bf)] + [shape((TOK,...  3.64 us
    ppermute x2, waiting for transfers between devices, body(): west.append(lax.ppermute(chunks[i], 'lon', forward))  1.79 us
    pallas_call x1, Pallas kernels, body(): pl.pallas_call(split_kernel, out_shape=[shape((rows, D), bf)] * NCH, in_s...  1.05 us
  transfers between devices with their start and end apart: 8, of which 2 were waited for; matrix products, arithmetic and copies ran while one was open for 0% of the time, Pallas kernels for 21%

profile of v1, /device:TPU:1, one launch (start us, length us, event | category | flops | bytes accessed | tf_op | source)
XLA Modules:
  0.0 47.6 jit_solution(13583382291028961389)
XLA Ops:
  0.0 0.0 copy-start
  0.0 1.1 %split.1 = (bf16[128,1024]{1,0:T(8,128)(2,1)S(1)}, bf16[128,1024]{1,0:T(8,128)(2,1)S(1)}) custom-call(bf16[256,1024]{1,0:T(8,128)(2,1)} %bitcast.2), custom_call_target="tpu_custom_call" | custom-call | tf_op jit(solution)/shard_map/split/pallas_call | solution.py:252
  1.1 11.3 %collective-permute-start.5 = (bf16[128,1024]{1,0:T(8,128)(2,1)S(1)}, bf16[128,1024]{1,0:T(8,128)(2,1)S(1)}, u32[]{:S(2)}, u32[]{:S(2)}) collective-permute-start(bf16[128,1024]{1,0:T(8,128)(2,1)S(1)} %get-tuple-element.39), channel_id=1, source_target_pairs={{1,0},{2,1},{3,2},{4,3},{5,4},{6,5},{7,6},{8,7},{9,8},{10,9},{11,1... | collective-permute-start | bytes 786440 | tf_op jit(solution)/shard_map/ppermute | solution.py:267
  12.4 0.0 collective-permute-start.4
  12.4 7.2 %collective-permute-start.1 = (bf16[128,1024]{1,0:T(8,128)(2,1)S(1)}, bf16[128,1024]{1,0:T(8,128)(2,1)S(1)}, u32[]{:S(2)}, u32[]{:S(2)}) collective-permute-start(bf16[128,1024]{1,0:T(8,128)(2,1)S(1)} %get-tuple-element.25), channel_id=1, source_target_pairs={{1,0},{2,1},{3,2},{4,3},{5,4},{6,5},{7,6},{8,7},{9,8},{10,9},{11,1... | collective-permute-start | bytes 786440 | tf_op jit(solution)/shard_map/ppermute | solution.py:267
  19.5 0.0 collective-permute-start
  19.6 0.0 copy-done
  19.6 3.6 %own.1 = (bf16[256,1024]{1,0:T(8,128)(2,1)S(1)}, bf16[256,512]{1,0:T(8,128)(2,1)S(1)}, bf16[256,512]{1,0:T(8,128)(2,1)S(1)}, bf16[256,512]{1,0:T(8,128)(2,1)S(1)...) custom-call(f32[6,1024]{1,0:T(8,128)S(1)} %copy-done, ...), custom_call_target="tpu_custom_call" | custom-call | tf_op jit(solution)/shard_map/own/pallas_call | solution.py:270
  23.2 0.0 collective-permute-done.5.east_ref
  23.2 1.8 %collective-permute-done.4.west_ref = bf16[128,1024]{1,0:T(8,128)(2,1)S(1)} collective-permute-done((bf16[128,1024]{1,0:T(8,128)(2,1)S(1)}, bf16[128,1024]{1,0:T(8,128)(2,1)S(1)}, u32[]{:S(2)}, u32[]{:S(2)}) %collective-permute-start.4) | collective-permute-done | bytes 262176 | tf_op jit(solution)/shard_map/ppermute | solution.py:265
  25.0 0.0 copy-start.1
  25.0 0.7 %copy-done.1 = s32[8,64]{1,0:T(8,128)S(1)} copy-done((s32[8,64]{1,0:T(8,128)S(1)}, s32[8,64]{1,0:T(8,128)}, u32[]{:S(2)}) %copy-start.1) | copy-done | bytes 2072
  25.7 3.2 %shard_map.110 = (bf16[128,1024]{1,0:T(8,128)(2,1)S(1)}, bf16[128,512]{1,0:T(8,128)(2,1)S(1)}, bf16[128,1024]{1,0:T(8,128)(2,1)S(1)}) custom-call(bf16[128,1024]{1,0:T(8,128)(2,1)S(1)} %collective-permute-done.4.west_ref, bf16[128,1024]{1,0:T(8,128)(2,1)S(1)} %collective-permute-done.5.east_ref, bf16[256,1024]{1,0:T(8,128)(2,1)S(1)} %get-tuple-element.26.x_ref, ...), custom_call_target="tpu_custom_call" | custom-call | tf_op jit(solution)/shard_map/pallas_call | solution.py:300
  28.9 4.0 %collective-permute-start.7 = (bf16[128,1024]{1,0:T(8,128)(2,1)S(1)}, bf16[128,1024]{1,0:T(8,128)(2,1)S(1)}, u32[]{:S(2)}, u32[]{:S(2)}) collective-permute-start(bf16[128,1024]{1,0:T(8,128)(2,1)S(1)} %get-tuple-element.41.refs_8_), channel_id=1, source_target_pairs={{64,128},{128,64},{65,129},{129,65},{66,130},{130,66},{67,131},{13... | collective-permute-start | bytes 786440 | tf_op jit(solution)/shard_map/ppermute | solution.py:307
  32.9 0.1 collective-permute-start.6
  33.0 0.0 collective-permute-done.1.east_ref
  33.0 0.0 collective-permute-done.west_ref
  33.0 3.2 %shard_map.109 = (bf16[128,1024]{1,0:T(8,128)(2,1)S(1)}, bf16[128,512]{1,0:T(8,128)(2,1)S(1)}, bf16[128,1024]{1,0:T(8,128)(2,1)S(1)}) custom-call(bf16[128,1024]{1,0:T(8,128)(2,1)S(1)} %collective-permute-done.west_ref, bf16[128,1024]{1,0:T(8,128)(2,1)S(1)} %collective-permute-done.1.east_ref, bf16[256,1024]{1,0:T(8,128)(2,1)S(1)} %get-tuple-element.26.x_ref, ...), custom_call_target="tpu_custom_call" | custom-call | tf_op jit(solution)/shard_map/pallas_call | solution.py:300
  36.1 3.2 %collective-permute-start.3 = (bf16[128,1024]{1,0:T(8,128)(2,1)S(1)}, bf16[128,1024]{1,0:T(8,128)(2,1)S(1)}, u32[]{:S(2)}, u32[]{:S(2)}) collective-permute-start(bf16[128,1024]{1,0:T(8,128)(2,1)S(1)} %get-tuple-element.37.refs_3_), channel_id=1, source_target_pairs={{64,128},{128,64},{65,129},{129,65},{66,130},{130,66},{67,131},{13... | collective-permute-start | bytes 786440 | tf_op jit(solution)/shard_map/ppermute | solution.py:307
  39.4 0.3 collective-permute-start.2
  39.6 0.0 collective-permute-done.7.refs_10_
  39.6 0.0 collective-permute-done.6.refs_9_
  39.7 4.2 %collective-permute-done.3.refs_5_ = bf16[128,1024]{1,0:T(8,128)(2,1)S(1)} collective-permute-done((bf16[128,1024]{1,0:T(8,128)(2,1)S(1)}, bf16[128,1024]{1,0:T(8,128)(2,1)S(1)}, u32[]{:S(2)}, u32[]{:S(2)}) %collective-permute-start.3) | collective-permute-done | bytes 262176 | tf_op jit(solution)/shard_map/ppermute | solution.py:307
  43.8 0.0 collective-permute-done.2.refs_4_
  43.8 3.8 %time.1 = bf16[256,1024]{1,0:T(8,128)(2,1)} custom-call(f32[6,1024]{1,0:T(8,128)S(1)} %copy-done, bf16[512,1024]{1,0:T(8,128)(2,1)S(1)} %get-tuple-element.24.refs_1_, bf16[128,512]{1,0:T(8,128)(2,1)S(1)} %get-tuple-element.36.refs_2_, bf16[128,1024]{1,0:T(8,128)(2,1)S(1)} %get-tuple-element.37.refs_3_, ...), custom_call_target="tpu_custom_call" | custom-call | tf_op jit(solution)/shard_map/time/pallas_call | solution.py:311
Async XLA Ops:
  0.0 19.6 %copy-start = (f32[6,1024]{1,0:T(8,128)S(1)}, f32[6,1024]{1,0:T(8,128)}, u32[]{:S(2)}) copy-start(f32[6,1024]{1,0:T(8,128)} %refs_0_.3) | copy-start | bytes 73732
  1.1 22.1 %collective-permute-start.5 = (bf16[128,1024]{1,0:T(8,128)(2,1)S(1)}, bf16[128,1024]{1,0:T(8,128)(2,1)S(1)}, u32[]{:S(2)}, u32[]{:S(2)}) collective-permute-start(bf16[128,1024]{1,0:T(8,128)(2,1)S(1)} %get-tuple-element.39), channel_id=1, source_target_pairs={{1,0},{2,1},{3,2},{4,3},{5,4},{6,5},{7,6},{8,7},{9,8},{10,9},{11,1... | collective-permute-start | bytes 786440 | tf_op jit(solution)/shard_map/ppermute | solution.py:267
  12.4 12.6 %collective-permute-start.4 = (bf16[128,1024]{1,0:T(8,128)(2,1)S(1)}, bf16[128,1024]{1,0:T(8,128)(2,1)S(1)}, u32[]{:S(2)}, u32[]{:S(2)}) collective-permute-start(bf16[128,1024]{1,0:T(8,128)(2,1)S(1)} %get-tuple-element.39), channel_id=1, source_target_pairs={{0,1},{1,2},{2,3},{3,4},{4,5},{5,6},{6,7},{7,8},{8,9},{9,10},{10,1... | collective-permute-start | bytes 786440 | tf_op jit(solution)/shard_map/ppermute | solution.py:265
  12.4 20.6 %collective-permute-start.1 = (bf16[128,1024]{1,0:T(8,128)(2,1)S(1)}, bf16[128,1024]{1,0:T(8,128)(2,1)S(1)}, u32[]{:S(2)}, u32[]{:S(2)}) collective-permute-start(bf16[128,1024]{1,0:T(8,128)(2,1)S(1)} %get-tuple-element.25), channel_id=1, source_target_pairs={{1,0},{2,1},{3,2},{4,3},{5,4},{6,5},{7,6},{8,7},{9,8},{10,9},{11,1... | collective-permute-start | bytes 786440 | tf_op jit(solution)/shard_map/ppermute | solution.py:267
  19.5 13.4 %collective-permute-start = (bf16[128,1024]{1,0:T(8,128)(2,1)S(1)}, bf16[128,1024]{1,0:T(8,128)(2,1)S(1)}, u32[]{:S(2)}, u32[]{:S(2)}) collective-permute-start(bf16[128,1024]{1,0:T(8,128)(2,1)S(1)} %get-tuple-element.25), channel_id=1, source_target_pairs={{0,1},{1,2},{2,3},{3,4},{4,5},{5,6},{6,7},{7,8},{8,9},{9,10},{10,1... | collective-permute-start | bytes 786440 | tf_op jit(solution)/shard_map/ppermute | solution.py:265
  25.0 0.7 %copy-start.1 = (s32[8,64]{1,0:T(8,128)S(1)}, s32[8,64]{1,0:T(8,128)}, u32[]{:S(2)}) copy-start(s32[8,64]{1,0:T(8,128)} %weight_ref.3) | copy-start | bytes 6148
  28.9 10.8 %collective-permute-start.7 = (bf16[128,1024]{1,0:T(8,128)(2,1)S(1)}, bf16[128,1024]{1,0:T(8,128)(2,1)S(1)}, u32[]{:S(2)}, u32[]{:S(2)}) collective-permute-start(bf16[128,1024]{1,0:T(8,128)(2,1)S(1)} %get-tuple-element.41.refs_8_), channel_id=1, source_target_pairs={{64,128},{128,64},{65,129},{129,65},{66,130},{130,66},{67,131},{13... | collective-permute-start | bytes 786440 | tf_op jit(solution)/shard_map/ppermute | solution.py:307
  32.9 6.8 %collective-permute-start.6 = (bf16[128,1024]{1,0:T(8,128)(2,1)S(1)}, bf16[128,1024]{1,0:T(8,128)(2,1)S(1)}, u32[]{:S(2)}, u32[]{:S(2)}) collective-permute-start(bf16[128,1024]{1,0:T(8,128)(2,1)S(1)} %get-tuple-element.41.refs_8_), channel_id=1, source_target_pairs={{0,64},{64,0},{128,192},{192,128},{1,65},{65,1},{129,193},{193,129... | collective-permute-start | bytes 786440 | tf_op jit(solution)/shard_map/ppermute | solution.py:308
  36.1 7.7 %collective-permute-start.3 = (bf16[128,1024]{1,0:T(8,128)(2,1)S(1)}, bf16[128,1024]{1,0:T(8,128)(2,1)S(1)}, u32[]{:S(2)}, u32[]{:S(2)}) collective-permute-start(bf16[128,1024]{1,0:T(8,128)(2,1)S(1)} %get-tuple-element.37.refs_3_), channel_id=1, source_target_pairs={{64,128},{128,64},{65,129},{129,65},{66,130},{130,66},{67,131},{13... | collective-permute-start | bytes 786440 | tf_op jit(solution)/shard_map/ppermute | solution.py:307
  39.4 4.5 %collective-permute-start.2 = (bf16[128,1024]{1,0:T(8,128)(2,1)S(1)}, bf16[128,1024]{1,0:T(8,128)(2,1)S(1)}, u32[]{:S(2)}, u32[]{:S(2)}) collective-permute-start(bf16[128,1024]{1,0:T(8,128)(2,1)S(1)} %get-tuple-element.37.refs_3_), channel_id=1, source_target_pairs={{0,64},{64,0},{128,192},{192,128},{1,65},{65,1},{129,193},{193,129... | collective-permute-start | bytes 786440 | tf_op jit(solution)/shard_map/ppermute | solution.py:308
